TPU v7x, 32 devices: a whole 2x2x4 slice. The times are simulated.
32 devices in a mesh: src: 4 (over y, x), dst: 8 (over z, core).
Axes of the slice: x: 2, y: 2, z: 4, core: 2. Of those that a mesh axis runs over, the one named last changes fastest.
Arguments:
- transition: bfloat16 [32768, 32768], P('src', 'dst'), may hold values from -0.046875 to 0.046875
- emit_cols: bfloat16 [16, 32768], P(None, 'dst'), may hold values from 0.25 to 4
- token_ids: int32 [48, 4], replicated, may hold values from 0 to 15
- alpha_start: bfloat16 [48, 32768], P(None, 'src'), may hold values from -6 to 6
- beta_end: bfloat16 [48, 32768], P(None, 'dst'), may hold values from -6 to 6
- inverse_likelihood: float32 [48], replicated, may hold values from 5 to 80
Outputs:
- counts: float32 [8192, 8192], P('src', 'dst')
Inputs may be any that keep to these rules, and one draw needn't show every extreme that they name: `token_ids`: each id selects one of the 16 supplied emission columns.
All inputs are finite; a program needn't handle non-finite values.
Results may differ from a plain program's by a relative error of at most 0.024.
Values may be sent and summed in bfloat16 or wider, within the bound.
No kernel may reach another device: no remote copies, remote signals or barrier semaphores. Data moves between devices by JAX's collectives and lax.ppermute only.
A program may use at most 128 MiB of HBM per device.

v0:
```python
import jax
import jax.numpy as jnp
from jax import lax
from jax.sharding import PartitionSpec as P

scaling = 0.75


def per_device(transition, emit_cols, token_ids, alpha_start, beta_end, inverse_likelihood):
    src_tile = transition.shape[0]
    dst_tile = transition.shape[1]
    src_count = lax.axis_size("src")
    dst_count = lax.axis_size("dst")
    tile_ratio = dst_count // src_count
    row_place = lax.axis_index("src")
    col_place = lax.axis_index("dst")
    seq_rows = alpha_start.shape[0]
    column_codes = lax.broadcasted_iota(jnp.int32, (1, emit_cols.shape[0]), 1)

    def emitted(position):
        selector = (token_ids[:, position : position + 1] == column_codes).astype(jnp.bfloat16)
        return jnp.dot(selector, emit_cols, preferred_element_type=jnp.float32)

    def forward(current, position):
        partial_value = jnp.dot(current, transition, preferred_element_type=jnp.float32)
        slice_width = dst_tile // src_count
        shared = lax.psum_scatter(
            partial_value.astype(jnp.bfloat16), "src", scatter_dimension=1, tiled=True
        ).astype(jnp.float32)
        emit_slice = lax.dynamic_slice_in_dim(
            emitted(position), row_place * slice_width, slice_width, 1
        )
        advanced = (scaling * emit_slice * shared).astype(jnp.bfloat16)
        spread = lax.all_gather(advanced, "dst", axis=1, tiled=True)
        shaped = spread.reshape(seq_rows, src_count, tile_ratio, 1, slice_width)
        regrouped = lax.all_to_all(shaped, "src", split_axis=1, concat_axis=3, tiled=True)
        return regrouped.reshape(seq_rows, src_tile)

    def backward(carried, position):
        partial_value = lax.dot_general(
            carried, transition, (((1,), (1,)), ((), ())), preferred_element_type=jnp.float32
        )
        slice_width = src_tile // dst_count
        shared = lax.psum_scatter(partial_value, "dst", scatter_dimension=1, tiled=True).astype(
            jnp.bfloat16
        )
        spread = lax.all_gather(shared, "src", axis=1, tiled=True)
        tiles = spread.reshape(seq_rows, src_count, 1, slice_width)
        outgoing = jnp.broadcast_to(tiles, (seq_rows, src_count, tile_ratio, slice_width)).reshape(
            seq_rows, dst_count, 1, slice_width
        )
        regrouped = lax.all_to_all(outgoing, "dst", split_axis=1, concat_axis=2, tiled=True)
        whole_tile = regrouped.reshape(seq_rows, src_tile)
        own_part = lax.dynamic_slice_in_dim(
            whole_tile, col_place % tile_ratio * dst_tile, dst_tile, 1
        )
        return (scaling * emitted(position) * own_part.astype(jnp.float32)).astype(jnp.bfloat16)

    alpha_one = forward(alpha_start, 0)
    alpha_two = forward(alpha_one, 1)
    message_four = (scaling * emitted(3) * beta_end.astype(jnp.float32)).astype(jnp.bfloat16)
    message_three = backward(message_four, 2)
    message_two = backward(message_three, 1)
    quarter_rows = src_tile // 4
    quarter_width = dst_tile // 4
    weights = inverse_likelihood[:, None]
    outer_sum = jnp.zeros((quarter_rows, quarter_width), jnp.float32)
    for alpha_rows, message in ((alpha_one, message_two), (alpha_two, message_three)):
        weighted = (weights * message[:, :quarter_width].astype(jnp.float32)).astype(jnp.bfloat16)
        outer_sum = outer_sum + lax.dot_general(
            alpha_rows[:, :quarter_rows],
            weighted,
            (((0,), (0,)), ((), ())),
            preferred_element_type=jnp.float32,
        )
    return transition[:quarter_rows, :quarter_width].astype(jnp.float32) * outer_sum


def solution(mesh):
    in_specs = (P("src", "dst"), P(None, "dst"), P(), P(None, "src"), P(None, "dst"), P())
    out_specs = P("src", "dst")
    return jax.shard_map(
        per_device, mesh=mesh, in_specs=in_specs, out_specs=out_specs, check_vma=False
    )
```

profile of v0, /device:TPU:0, one launch (start us, length us, event | category | flops | bytes accessed | tf_op | source)
XLA Modules:
  0.0 261.0 jit_solution(8276515694606811173)
XLA Ops:
  6.5 0.0 copy-start
  6.5 0.0 copy-start.4
  6.5 0.0 copy-start.2
  6.5 0.0 copy-start.1
  6.5 0.0 reduce-scatter.5.cloned.1.call-start
  6.6 1.1 copy-done
  7.7 24.1 %convolution_convert_fusion.1 = bf16[48,4096]{1,0:T(8,128)(2,1)} fusion(bf16[48,8192]{1,0:T(8,128)(2,1)S(1)} %copy-done, bf16[8192,4096]{1,0:T(8,128)(2,1)} %param.6), kind=kOutput, calls=%fused_computation.8 | convolution fusion | flops 3221422080 | bytes 68288512 | tf_op jit(solution)/shard_map/dot_general | solution.py:25
  31.8 0.0 reduce-scatter.5.cloned.1.call-update
  31.8 0.0 reduce-scatter.7.cloned.1.call-start
  31.9 0.0 copy-done.4
  31.9 0.0 copy-done.2
  31.9 0.0 copy-done.1
  31.9 30.0 %fusion.4 = f32[48,8192]{1,0:T(8,128)} fusion(bf16[8192,4096]{1,0:T(8,128)(2,1)} %param.6, bf16[16,4096]{1,0:T(8,128)(2,1)S(1)} %copy-done.1, bf16[48,4096]{1,0:T(8,128)(2,1)S(1)} %copy-done.2, s32[48]{0:T(128)S(1)} %get-tuple-element.8), kind=kOutput, calls=%fused_computation.9 | convolution fusion | flops 3228304128 | bytes 69206208 | tf_op jit(solution)/shard_map/dot_general | solution.py:40
  62.0 0.0 reduce-scatter.7.cloned.1.call-update
  62.0 0.3 fusion.18
  62.3 0.0 reduce-scatter.5.cloned.1.call-done
  62.3 0.9 multiply_convert_fusion.3
  63.3 20.5 %all_gather.12 = bf16[48,8192]{1,0:T(8,128)(2,1)S(1)} all-gather(bf16[48,1024]{1,0:T(8,128)(2,1)S(1)} %multiply_convert_fusion.3), channel_id=1, replica_groups=mesh['src'=4,'dst'=8] {'dst'}, dimensions={1}, use_global_device_ids=true | all-gather | bytes 884736 | tf_op jit(solution)/shard_map/all_gather | solution.py:34
  83.8 0.6 reshape.39
  84.4 1.5 copy.9
  85.8 3.8 %all-to-all-start = ((bf16[48,4,2,1,1024]{4,2,0,3,1:T(2,128)(2,1)}), bf16[48,4,2,1,1024]{4,2,0,3,1:T(2,128)(2,1)S(1)}, u32[]{:S(2)}, u32[]{:S(2)}) async-start(bf16[48,4,2,1,1024]{4,2,0,3,1:T(2,128)(2,1)} %copy.9), calls=%async_computation.1 | async-start | bytes 1572864 | tf_op jit(solution)/shard_map/all_to_all | solution.py:36
  89.6 11.3 %all-to-all-done = bf16[48,4,2,1,1024]{4,2,0,3,1:T(2,128)(2,1)S(1)} async-done(((bf16[48,4,2,1,1024]{4,2,0,3,1:T(2,128)(2,1)}), bf16[48,4,2,1,1024]{4,2,0,3,1:T(2,128)(2,1)S(1)}, u32[]{:S(2)}, u32[]{:S(2)}) %all-to-all-start) | async-done | bytes 786464 | tf_op jit(solution)/shard_map/all_to_all | solution.py:36
  100.9 0.6 copy.10
  101.5 0.6 reshape.40
  102.1 0.0 reduce-scatter.7.cloned.1.call-done
  102.1 0.9 convert_element_type.68
  103.1 9.9 %all_gather.13 = bf16[48,4096]{1,0:T(8,128)(2,1)S(1)} all-gather(bf16[48,1024]{1,0:T(8,128)(2,1)S(1)} %convert_element_type.68), channel_id=1, replica_groups=mesh['src'=4,'dst'=8] {'src'}, dimensions={1}, use_global_device_ids=true | all-gather | bytes 491520 | tf_op jit(solution)/shard_map/all_gather | solution.py:47
  113.0 1.0 broadcast_in_dim.16
  114.0 3.9 %all-to-all-start.1 = ((bf16[48,8,1,1024]{3,0,2,1:T(8,128)(2,1)}), bf16[48,8,1,1024]{3,0,2,1:T(8,128)(2,1)S(1)}, u32[]{:S(2)}, u32[]{:S(2)}) async-start(bf16[48,8,1,1024]{3,0,2,1:T(8,128)(2,1)} %bitcast.6), calls=%async_computation.3 | async-start | bytes 1572864 | tf_op jit(solution)/shard_map/all_to_all | solution.py:52
  117.9 0.0 copy-start.3
  117.9 0.0 reduce-scatter.11.cloned.1.call-start
  117.9 24.1 %convolution_convert_fusion = bf16[48,4096]{1,0:T(8,128)(2,1)} fusion(bf16[48,8192]{1,0:T(8,128)(2,1)S(1)} %reshape.40, bf16[8192,4096]{1,0:T(8,128)(2,1)} %param.6), kind=kOutput, calls=%fused_computation.7 | convolution fusion | flops 3221422080 | bytes 68288512 | tf_op jit(solution)/shard_map/dot_general | solution.py:25
  142.1 0.0 reduce-scatter.11.cloned.1.call-update
  142.1 0.2 reduce-scatter.9.cloned.1.call-start
  142.3 0.0 all-to-all-done.1
  142.3 0.1 copy.19
  142.4 0.3 fusion.2
  142.7 29.5 %fusion.28 = f32[48,8192]{1,0:T(8,128)} fusion(bf16[48,4096]{1,0:T(8,128)(2,1)S(1)} %fusion.2, bf16[8192,4096]{1,0:T(8,128)(2,1)} %param.6), kind=kOutput, calls=%fused_computation.46 | convolution fusion | flops 3221225472 | bytes 69074944 | tf_op jit(solution)/shard_map/dot_general | solution.py:40
  172.2 0.0 reduce-scatter.9.cloned.1.call-update
  172.2 1.2 fusion.19
  173.5 0.0 reduce-scatter.11.cloned.1.call-done
  173.5 1.0 multiply_convert_fusion.1
  174.5 20.2 %all_gather.15 = bf16[48,8192]{1,0:T(8,128)(2,1)S(1)} all-gather(bf16[48,1024]{1,0:T(8,128)(2,1)S(1)} %multiply_convert_fusion.1), channel_id=1, replica_groups=mesh['src'=4,'dst'=8] {'dst'}, dimensions={1}, use_global_device_ids=true | all-gather | bytes 884736 | tf_op jit(solution)/shard_map/all_gather | solution.py:34
  194.7 0.6 reshape.45
  195.2 1.5 copy.15
  196.7 3.5 %all-to-all-start.3 = ((bf16[48,4,2,1,1024]{4,2,0,3,1:T(2,128)(2,1)}), bf16[48,4,2,1,1024]{4,2,0,3,1:T(2,128)(2,1)S(1)}, u32[]{:S(2)}, u32[]{:S(2)}) async-start(bf16[48,4,2,1,1024]{4,2,0,3,1:T(2,128)(2,1)} %copy.15), calls=%async_computation.7 | async-start | bytes 1572864 | tf_op jit(solution)/shard_map/all_to_all | solution.py:36
  200.2 9.3 %reduce-scatter.9.cloned.1.call-done = f32[48,1024]{1,0:T(8,128)} async-done(((f32[48,8192]{1,0:T(8,128)}), f32[48,1024]{1,0:T(8,128)}) %reduce-scatter.9.cloned.1.call-update) | async-done | bytes 196624 | tf_op jit(solution)/shard_map/reduce_scatter | solution.py:44
  209.5 0.9 convert_element_type.71
  210.4 9.3 %all_gather.14 = bf16[48,4096]{1,0:T(8,128)(2,1)S(1)} all-gather(bf16[48,1024]{1,0:T(8,128)(2,1)S(1)} %convert_element_type.71), channel_id=1, replica_groups=mesh['src'=4,'dst'=8] {'src'}, dimensions={1}, use_global_device_ids=true | all-gather | bytes 491520 | tf_op jit(solution)/shard_map/all_gather | solution.py:47
  219.8 0.0 all-to-all-done.3
  219.8 1.0 broadcast_in_dim.18
  220.8 3.5 %all-to-all-start.2 = ((bf16[48,8,1,1024]{3,0,2,1:T(8,128)(2,1)}), bf16[48,8,1,1024]{3,0,2,1:T(8,128)(2,1)S(1)}, u32[]{:S(2)}, u32[]{:S(2)}) async-start(bf16[48,8,1,1024]{3,0,2,1:T(8,128)(2,1)} %bitcast.53), calls=%async_computation.5 | async-start | bytes 1572864 | tf_op jit(solution)/shard_map/all_to_all | solution.py:52
  224.3 1.5 copy.16
  225.9 2.1 reshape.46
  228.0 17.2 %all-to-all-done.2 = bf16[48,8,1,1024]{3,0,2,1:T(8,128)(2,1)S(1)} async-done(((bf16[48,8,1,1024]{3,0,2,1:T(8,128)(2,1)}), bf16[48,8,1,1024]{3,0,2,1:T(8,128)(2,1)S(1)}, u32[]{:S(2)}, u32[]{:S(2)}) %all-to-all-start.2) | async-done | bytes 786464 | tf_op jit(solution)/shard_map/all_to_all | solution.py:52
  245.2 0.1 copy.20
  245.3 0.0 copy-done.3
  245.3 2.2 fusion.10
  247.5 6.9 %add_multiply_fusion = f32[2048,1024]{1,0:T(8,128)} fusion(f32[2048,1024]{1,0:T(8,128)S(1)} %fusion.10, bf16[8192,4096]{1,0:T(8,128)(2,1)} %param.6, bf16[48,8192]{1,0:T(8,128)(2,1)S(1)} %reshape.46, bf16[48,4096]{1,0:T(8,128)(2,1)S(1)} %fusion.2, f32[48]{0:T(128)S(1)} %copy-done.3), kind=kOutput, calls=%fused_computation | convolution fusion | flops 207765504 | bytes 21266944 | tf_op jit(solution)/shard_map/dot_general | solution.py:70
  (3 shorter events, 0.1 us)
Async XLA Ops:
  6.5 1.1 copy-start
  6.5 25.3 %copy-start.4 = (s32[48,4]{0,1:T(4,128)S(1)}, s32[48,4]{0,1:T(4,128)}, u32[]{:S(2)}) copy-start(s32[48,4]{0,1:T(4,128)} %param.8) | copy-start | bytes 2308
  6.5 25.4 %copy-start.2 = (bf16[48,4096]{1,0:T(8,128)(2,1)S(1)}, bf16[48,4096]{1,0:T(8,128)(2,1)}, u32[]{:S(2)}) copy-start(bf16[48,4096]{1,0:T(8,128)(2,1)} %param.10) | copy-start | bytes 1179652
  6.5 25.4 %copy-start.1 = (bf16[16,4096]{1,0:T(8,128)(2,1)S(1)}, bf16[16,4096]{1,0:T(8,128)(2,1)}, u32[]{:S(2)}) copy-start(bf16[16,4096]{1,0:T(8,128)(2,1)} %param.7) | copy-start | bytes 393220
  6.5 55.8 %reduce-scatter.5.cloned.1.call-start = ((), (), s32[]{:S(2)}) async-start(), calls=%async_computation.8 | async-start | bytes 491520 | tf_op jit(solution)/shard_map/reduce_scatter | solution.py:27
  31.8 70.3 %reduce-scatter.7.cloned.1.call-start = ((), (), s32[]{:S(2)}) async-start(), calls=%async_computation.9 | async-start | bytes 1769472 | tf_op jit(solution)/shard_map/reduce_scatter | solution.py:44
  85.8 15.1 %all-to-all-start = ((bf16[48,4,2,1,1024]{4,2,0,3,1:T(2,128)(2,1)}), bf16[48,4,2,1,1024]{4,2,0,3,1:T(2,128)(2,1)S(1)}, u32[]{:S(2)}, u32[]{:S(2)}) async-start(bf16[48,4,2,1,1024]{4,2,0,3,1:T(2,128)(2,1)} %copy.9), calls=%async_computation.1 | async-start | bytes 1572864 | tf_op jit(solution)/shard_map/all_to_all | solution.py:36
  114.0 28.3 %all-to-all-start.1 = ((bf16[48,8,1,1024]{3,0,2,1:T(8,128)(2,1)}), bf16[48,8,1,1024]{3,0,2,1:T(8,128)(2,1)S(1)}, u32[]{:S(2)}, u32[]{:S(2)}) async-start(bf16[48,8,1,1024]{3,0,2,1:T(8,128)(2,1)} %bitcast.6), calls=%async_computation.3 | async-start | bytes 1572864 | tf_op jit(solution)/shard_map/all_to_all | solution.py:52
  117.9 127.4 %copy-start.3 = (f32[48]{0:T(128)S(1)}, f32[48]{0:T(128)}, u32[]{:S(2)}) copy-start(f32[48]{0:T(128)} %param.11) | copy-start | bytes 580
  117.9 55.6 %reduce-scatter.11.cloned.1.call-start = ((), (), s32[]{:S(2)}) async-start(), calls=%async_computation.11 | async-start | bytes 491520 | tf_op jit(solution)/shard_map/reduce_scatter | solution.py:27
  142.1 67.4 %reduce-scatter.9.cloned.1.call-start = ((), (), s32[]{:S(2)}) async-start(), calls=%async_computation.10 | async-start | bytes 1769472 | tf_op jit(solution)/shard_map/reduce_scatter | solution.py:44
  196.7 23.1 %all-to-all-start.3 = ((bf16[48,4,2,1,1024]{4,2,0,3,1:T(2,128)(2,1)}), bf16[48,4,2,1,1024]{4,2,0,3,1:T(2,128)(2,1)S(1)}, u32[]{:S(2)}, u32[]{:S(2)}) async-start(bf16[48,4,2,1,1024]{4,2,0,3,1:T(2,128)(2,1)} %copy.15), calls=%async_computation.7 | async-start | bytes 1572864 | tf_op jit(solution)/shard_map/all_to_all | solution.py:36
  220.8 24.4 %all-to-all-start.2 = ((bf16[48,8,1,1024]{3,0,2,1:T(8,128)(2,1)}), bf16[48,8,1,1024]{3,0,2,1:T(8,128)(2,1)S(1)}, u32[]{:S(2)}, u32[]{:S(2)}) async-start(bf16[48,8,1,1024]{3,0,2,1:T(8,128)(2,1)} %bitcast.53), calls=%async_computation.5 | async-start | bytes 1572864 | tf_op jit(solution)/shard_map/all_to_all | solution.py:52
Sparse Core Ops, SparseCore 0:
  31.9 27.4 reduce-scatter.4
  62.1 38.2 reduce-scatter.6
  142.2 25.1 reduce-scatter.10
  172.4 37.0 reduce-scatter.8
where the time goes:
time: 262 us; the launch traced here: 261 us
  matrix products  119 us (45%)
  blocking collectives  59.9 us (23%)
  waiting for transfers between devices  38 us (15%)
  starting transfers between devices  15 us (6%)
  between operations  13.3 us (5%)
  local copies, waits for them, and re-layouts  12.1 us (5%)
  other arithmetic  3.8 us (1%)
    dot_general x2, matrix products, backward(): lax.dot_general(carried, transition, (((1,), (1,)), ((), ())), preferred_...  59.6 us
    dot_general x2, matrix products, forward(): jnp.dot(current, transition, preferred_element_type=jnp.float32)  48.3 us
    all_gather x2, blocking collectives, forward(): spread = lax.all_gather(advanced, 'dst', axis=1, tiled=True)  40.7 us
    all_gather x2, blocking collectives, backward(): spread = lax.all_gather(shared, 'src', axis=1, tiled=True)  19.2 us
    all_to_all x2, waiting for transfers between devices, backward(): lax.all_to_all(outgoing, 'dst', split_axis=1, concat_axis=2, tiled=True)  17.2 us
    all_to_all x2, waiting for transfers between devices, forward(): lax.all_to_all(shaped, 'src', split_axis=1, concat_axis=3, tiled=True)  11.3 us
    reduce_scatter x2, waiting for transfers between devices, backward(): lax.psum_scatter(partial_value, 'dst', scatter_dimension=1, tiled=True)  9.31 us
    dot_general x2, matrix products, per_device(): lax.dot_general(alpha_rows[:, :quarter_rows], weighted, (((0,), (0,)), ((...  9.17 us
  transfers between devices with their start and end apart: 8, of which 3 were waited for; matrix products, arithmetic and copies ran while one was open for 37% of the time, Pallas kernels for 0%

commit v1 on v0

--- a/solution.py
+++ b/solution.py
@@ -44,7 +44,14 @@
         shared = lax.psum_scatter(partial_value, "dst", scatter_dimension=1, tiled=True).astype(
             jnp.bfloat16
         )
-        spread = lax.all_gather(shared, "src", axis=1, tiled=True)
+        ring = [shared]
+        for hop in range(3):
+            ring.append(lax.ppermute(ring[-1], "src", [(dev, (dev + 1) % 4) for dev in range(4)]))
+        spread = jnp.roll(
+            jnp.concatenate(ring[::-1], axis=1),
+            (lax.axis_index("src") + 1) * ring[0].shape[1],
+            axis=1,
+        )
         tiles = spread.reshape(seq_rows, src_count, 1, slice_width)
         outgoing = jnp.broadcast_to(tiles, (seq_rows, src_count, tile_ratio, slice_width)).reshape(
             seq_rows, dst_count, 1, slice_width

time: 262 us -> 345 us (1.32)
  waiting for transfers between devices: 38 us -> 141 us
  blocking collectives: 59.9 us -> 30.9 us
  starting transfers between devices: 15 us -> 22.7 us
    reduce_scatter x2, waiting for transfers between devices: 0.02 us -> 48.3 us  [forward(): lax.psum_scatter(partial_value.astype(jnp.bfloat16), 'src', scatter_dimen...]
    reduce_scatter x2, waiting for transfers between devices: 9.31 us -> 46.7 us  [backward(): lax.psum_scatter(partial_value, 'dst', scatter_dimension=1, tiled=True)]
    ppermute x0 -> x6, waiting for transfers between devices: none -> 28.7 us  [backward(): lax.ppermute(ring[-1], 'src', [(dev, (dev + 1) % 4) for dev in range(4)])]
    all_gather x2 -> x0, blocking collectives: 19.2 us -> none  [backward(): spread = lax.all_gather(shared, 'src', axis=1, tiled=True)]
    all_to_all x2, waiting for transfers between devices: 11.3 us -> 0.01 us  [forward(): lax.all_to_all(shaped, 'src', split_axis=1, concat_axis=3, tiled=True)]
    all_gather x2, blocking collectives: 40.7 us -> 30.9 us  [forward(): spread = lax.all_gather(advanced, 'dst', axis=1, tiled=True)]
    ppermute x0 -> x6, starting transfers between devices: none -> 6.91 us  [backward(): lax.ppermute(ring[-1], 'src', [(dev, (dev + 1) % 4) for dev in range(4)])]
  transfers between devices with their start and end apart: 8 -> 14, of which waited for: 3 -> 9; matrix products, arithmetic and copies ran while one was open for 37% -> 27% of each run, Pallas kernels for 0% -> 0%
where the time goes in v1:
time: 345 us; the launch traced here: 344 us
  waiting for transfers between devices  141 us (41%)
  matrix products  117 us (34%)
  blocking collectives  30.9 us (9%)
  starting transfers between devices  22.7 us (7%)
  between operations  14.8 us (4%)
  local copies, waits for them, and re-layouts  11.8 us (3%)
  other arithmetic  6.1 us (2%)
    dot_general x2, matrix products, backward(): lax.dot_general(carried, transition, (((1,), (1,)), ((), ())), preferred_...  58.1 us
    dot_general x2, matrix products, forward(): jnp.dot(current, transition, preferred_element_type=jnp.float32)  48.7 us
    reduce_scatter x2, waiting for transfers between devices, forward(): lax.psum_scatter(partial_value.astype(jnp.bfloat16), 'src', scatter_dimen...  48.3 us
    reduce_scatter x2, waiting for transfers between devices, backward(): lax.psum_scatter(partial_value, 'dst', scatter_dimension=1, tiled=True)  46.7 us
    all_gather x2, blocking collectives, forward(): spread = lax.all_gather(advanced, 'dst', axis=1, tiled=True)  30.9 us
    ppermute x6, waiting for transfers between devices, backward(): lax.ppermute(ring[-1], 'src', [(dev, (dev + 1) % 4) for dev in range(4)])  28.7 us
    all_to_all x2, waiting for transfers between devices, backward(): lax.all_to_all(outgoing, 'dst', split_axis=1, concat_axis=2, tiled=True)  17.3 us
    dot_general x2, matrix products, per_device(): lax.dot_general(alpha_rows[:, :quarter_rows], weighted, (((0,), (0,)), ((...  9.24 us
  transfers between devices with their start and end apart: 14, of which 9 were waited for; matrix products, arithmetic and copies ran while one was open for 27% of the time, Pallas kernels for 0%

profile of v1, /device:TPU:0, one launch (start us, length us, event | category | flops | bytes accessed | tf_op | source)
XLA Modules:
  0.0 344.4 jit_solution(3513803292428302613)
XLA Ops:
  7.4 0.0 copy-start
  7.4 0.8 slice_bitcast_fusion.1
  8.2 28.6 %fusion.4 = f32[48,8192]{1,0:T(8,128)} fusion(bf16[8192,4096]{1,0:T(8,128)(2,1)} %param.8, bf16[16,4096]{1,0:T(8,128)(2,1)} %param.9, bf16[48,4096]{1,0:T(8,128)(2,1)} %param.12, s32[48]{0:T(128)S(1)} %get-tuple-element.9), kind=kOutput, calls=%fused_computation.9 | convolution fusion | flops 3228304128 | bytes 69206208 | tf_op jit(solution)/shard_map/dot_general | solution.py:40
  36.8 0.0 reduce-scatter.7.cloned.1.call-update
  36.8 37.0 %reduce-scatter.7.cloned.1.call-done = f32[48,1024]{1,0:T(8,128)} async-done(((f32[48,8192]{1,0:T(8,128)}), f32[48,1024]{1,0:T(8,128)}) %reduce-scatter.7.cloned.1.call-update) | async-done | bytes 196624 | tf_op jit(solution)/shard_map/reduce_scatter | solution.py:44
  73.8 0.9 convert_element_type.68
  74.8 1.7 collective-permute-start
  76.4 4.8 %collective-permute-done = bf16[48,1024]{1,0:T(8,128)(2,1)S(1)} collective-permute-done((bf16[48,1024]{1,0:T(8,128)(2,1)S(1)}, bf16[48,1024]{1,0:T(8,128)(2,1)S(1)}, u32[]{:S(2)}, u32[]{:S(2)}) %collective-permute-start) | collective-permute-done | bytes 98336 | tf_op jit(solution)/shard_map/ppermute | solution.py:49
  81.3 0.0 collective-permute-start.1
  81.3 5.7 %collective-permute-done.1 = bf16[48,1024]{1,0:T(8,128)(2,1)S(1)} collective-permute-done((bf16[48,1024]{1,0:T(8,128)(2,1)S(1)}, bf16[48,1024]{1,0:T(8,128)(2,1)S(1)}, u32[]{:S(2)}, u32[]{:S(2)}) %collective-permute-start.1) | collective-permute-done | bytes 98336 | tf_op jit(solution)/shard_map/ppermute | solution.py:49
  87.0 0.0 collective-permute-start.2
  87.0 5.5 %collective-permute-done.2 = bf16[48,1024]{1,0:T(8,128)(2,1)S(1)} collective-permute-done((bf16[48,1024]{1,0:T(8,128)(2,1)S(1)}, bf16[48,1024]{1,0:T(8,128)(2,1)S(1)}, u32[]{:S(2)}, u32[]{:S(2)}) %collective-permute-start.2) | collective-permute-done | bytes 98336 | tf_op jit(solution)/shard_map/ppermute | solution.py:49
  92.5 0.8 fusion.16
  93.4 1.0 broadcast_in_dim.16
  94.3 3.5 %all-to-all-start.1 = ((bf16[48,8,1,1024]{3,0,2,1:T(8,128)(2,1)}), bf16[48,8,1,1024]{3,0,2,1:T(8,128)(2,1)S(1)}, u32[]{:S(2)}, u32[]{:S(2)}) async-start(bf16[48,8,1,1024]{3,0,2,1:T(8,128)(2,1)} %bitcast.6), calls=%async_computation.3 | async-start | bytes 1572864 | tf_op jit(solution)/shard_map/all_to_all | solution.py:59
  97.9 0.0 reduce-scatter.5.cloned.1.call-start
  98.0 0.0 copy-done
  98.0 24.2 %convolution_convert_fusion.1 = bf16[48,4096]{1,0:T(8,128)(2,1)} fusion(bf16[48,8192]{1,0:T(8,128)(2,1)S(1)} %copy-done, bf16[8192,4096]{1,0:T(8,128)(2,1)} %param.8), kind=kOutput, calls=%fused_computation.8 | convolution fusion | flops 3221422080 | bytes 68288512 | tf_op jit(solution)/shard_map/dot_general | solution.py:25
  122.1 0.0 reduce-scatter.5.cloned.1.call-update
  122.2 0.3 fusion.32
  122.5 25.0 %reduce-scatter.5.cloned.1.call-done = bf16[48,1024]{1,0:T(8,128)(2,1)} async-done(((bf16[48,4096]{1,0:T(8,128)(2,1)}), bf16[48,1024]{1,0:T(8,128)(2,1)}) %reduce-scatter.5.cloned.1.call-update) | async-done | bytes 98320 | tf_op jit(solution)/shard_map/reduce_scatter | solution.py:27
  147.5 0.9 multiply_convert_fusion.3
  148.4 15.5 %all_gather.6 = bf16[48,8192]{1,0:T(8,128)(2,1)S(1)} all-gather(bf16[48,1024]{1,0:T(8,128)(2,1)S(1)} %multiply_convert_fusion.3), channel_id=1, replica_groups=mesh['src'=4,'dst'=8] {'dst'}, dimensions={1}, use_global_device_ids=true | all-gather | bytes 884736 | tf_op jit(solution)/shard_map/all_gather | solution.py:34
  163.9 0.6 reshape.39
  164.5 1.4 copy.15
  165.9 0.0 all-to-all-done.1
  165.9 3.5 %all-to-all-start = ((bf16[48,4,2,1,1024]{4,2,0,3,1:T(2,128)(2,1)}), bf16[48,4,2,1,1024]{4,2,0,3,1:T(2,128)(2,1)S(1)}, u32[]{:S(2)}, u32[]{:S(2)}) async-start(bf16[48,4,2,1,1024]{4,2,0,3,1:T(2,128)(2,1)} %copy.15), calls=%async_computation.1 | async-start | bytes 1572864 | tf_op jit(solution)/shard_map/all_to_all | solution.py:36
  169.4 0.0 reduce-scatter.9.cloned.1.call-start
  169.5 0.1 copy.25
  169.5 0.3 fusion.2
  169.9 0.0 copy-start.4
  169.9 29.6 %fusion.42 = f32[48,8192]{1,0:T(8,128)} fusion(bf16[48,4096]{1,0:T(8,128)(2,1)S(1)} %fusion.2, bf16[8192,4096]{1,0:T(8,128)(2,1)} %param.8), kind=kOutput, calls=%fused_computation.76 | convolution fusion | flops 3221225472 | bytes 69074944 | tf_op jit(solution)/shard_map/dot_general | solution.py:40
  199.5 0.0 reduce-scatter.9.cloned.1.call-update
  199.5 0.2 reduce-scatter.11.cloned.1.call-start
  199.7 0.0 all-to-all-done
  199.7 0.6 copy.16
  200.3 0.6 reshape.40
  200.9 24.6 %convolution_convert_fusion = bf16[48,4096]{1,0:T(8,128)(2,1)} fusion(bf16[48,8192]{1,0:T(8,128)(2,1)S(1)} %reshape.40, bf16[8192,4096]{1,0:T(8,128)(2,1)} %param.8), kind=kOutput, calls=%fused_computation.7 | convolution fusion | flops 3221422080 | bytes 68288512 | tf_op jit(solution)/shard_map/dot_general | solution.py:25
  225.5 0.0 reduce-scatter.11.cloned.1.call-update
  225.5 0.3 fusion.33
  225.8 9.6 %reduce-scatter.9.cloned.1.call-done = f32[48,1024]{1,0:T(8,128)} async-done(((f32[48,8192]{1,0:T(8,128)}), f32[48,1024]{1,0:T(8,128)}) %reduce-scatter.9.cloned.1.call-update) | async-done | bytes 196624 | tf_op jit(solution)/shard_map/reduce_scatter | solution.py:44
  235.5 0.9 convert_element_type.71
  236.4 1.7 collective-permute-start.3
  238.1 23.2 %reduce-scatter.11.cloned.1.call-done = bf16[48,1024]{1,0:T(8,128)(2,1)} async-done(((bf16[48,4096]{1,0:T(8,128)(2,1)}), bf16[48,1024]{1,0:T(8,128)(2,1)}) %reduce-scatter.11.cloned.1.call-update) | async-done | bytes 98320 | tf_op jit(solution)/shard_map/reduce_scatter | solution.py:27
  261.4 0.9 multiply_convert_fusion.1
  262.3 0.0 collective-permute-done.3
  262.3 1.5 collective-permute-start.4
  263.8 15.5 %all_gather.7 = bf16[48,8192]{1,0:T(8,128)(2,1)S(1)} all-gather(bf16[48,1024]{1,0:T(8,128)(2,1)S(1)} %multiply_convert_fusion.1), channel_id=1, replica_groups=mesh['src'=4,'dst'=8] {'dst'}, dimensions={1}, use_global_device_ids=true | all-gather | bytes 884736 | tf_op jit(solution)/shard_map/all_gather | solution.py:34
  279.3 0.6 reshape.45
  279.9 1.4 copy.21
  281.3 3.5 %all-to-all-start.3 = ((bf16[48,4,2,1,1024]{4,2,0,3,1:T(2,128)(2,1)}), bf16[48,4,2,1,1024]{4,2,0,3,1:T(2,128)(2,1)S(1)}, u32[]{:S(2)}, u32[]{:S(2)}) async-start(bf16[48,4,2,1,1024]{4,2,0,3,1:T(2,128)(2,1)} %copy.21), calls=%async_computation.7 | async-start | bytes 1572864 | tf_op jit(solution)/shard_map/all_to_all | solution.py:36
  284.8 0.0 collective-permute-done.4
  284.8 2.0 collective-permute-start.5
  286.8 12.6 %collective-permute-done.5 = bf16[48,1024]{1,0:T(8,128)(2,1)S(1)} collective-permute-done((bf16[48,1024]{1,0:T(8,128)(2,1)}, bf16[48,1024]{1,0:T(8,128)(2,1)S(1)}, u32[]{:S(2)}, u32[]{:S(2)}) %collective-permute-start.5) | collective-permute-done | bytes 98336 | tf_op jit(solution)/shard_map/ppermute | solution.py:49
  299.4 1.6 fusion.9
  301.0 0.0 all-to-all-done.3
  301.0 1.0 broadcast_in_dim.18
  302.0 5.0 %all-to-all-start.2 = ((bf16[48,8,1,1024]{3,0,2,1:T(8,128)(2,1)}), bf16[48,8,1,1024]{3,0,2,1:T(8,128)(2,1)S(1)}, u32[]{:S(2)}, u32[]{:S(2)}) async-start(bf16[48,8,1,1024]{3,0,2,1:T(8,128)(2,1)} %bitcast.53), calls=%async_computation.5 | async-start | bytes 1572864 | tf_op jit(solution)/shard_map/all_to_all | solution.py:59
  307.0 1.5 copy.22
  308.5 2.1 reshape.46
  310.6 17.3 %all-to-all-done.2 = bf16[48,8,1,1024]{3,0,2,1:T(8,128)(2,1)S(1)} async-done(((bf16[48,8,1,1024]{3,0,2,1:T(8,128)(2,1)}), bf16[48,8,1,1024]{3,0,2,1:T(8,128)(2,1)S(1)}, u32[]{:S(2)}, u32[]{:S(2)}) %all-to-all-start.2) | async-done | bytes 786464 | tf_op jit(solution)/shard_map/all_to_all | solution.py:59
  327.9 0.1 copy.26
  328.0 2.2 fusion.24
  330.2 7.0 %add_multiply_fusion = f32[2048,1024]{1,0:T(8,128)} fusion(f32[2048,1024]{1,0:T(8,128)S(1)} %fusion.24, bf16[8192,4096]{1,0:T(8,128)(2,1)} %param.8, bf16[48,8192]{1,0:T(8,128)(2,1)S(1)} %reshape.46, bf16[48,4096]{1,0:T(8,128)(2,1)} %copy-done.2, f32[48]{0:T(128)S(1)} %copy-done.4), kind=kOutput, calls=%fused_computation | convolution fusion | flops 207765504 | bytes 21266944 | tf_op jit(solution)/shard_map/dot_general | solution.py:77
  (10 shorter events, 0.1 us)
Async XLA Ops:
  7.4 90.6 %copy-start = (bf16[48,8192]{1,0:T(8,128)(2,1)S(1)}, bf16[48,8192]{1,0:T(8,128)(2,1)}, u32[]{:S(2)}) copy-start(bf16[48,8192]{1,0:T(8,128)(2,1)} %param.11) | copy-start | bytes 2359300
  7.4 66.5 %reduce-scatter.7.cloned.1.call-start = ((), (), s32[]{:S(2)}) async-start(), calls=%async_computation.9 | async-start | bytes 1769472 | tf_op jit(solution)/shard_map/reduce_scatter | solution.py:44
  8.2 113.9 %copy-start.1 = (bf16[16,4096]{1,0:T(8,128)(2,1)S(1)}, bf16[16,4096]{1,0:T(8,128)(2,1)}, u32[]{:S(2)}) copy-start(bf16[16,4096]{1,0:T(8,128)(2,1)} %param.9) | copy-start | bytes 393220
  74.8 6.5 %collective-permute-start = (bf16[48,1024]{1,0:T(8,128)(2,1)S(1)}, bf16[48,1024]{1,0:T(8,128)(2,1)S(1)}, u32[]{:S(2)}, u32[]{:S(2)}) collective-permute-start(bf16[48,1024]{1,0:T(8,128)(2,1)S(1)} %convert_element_type.68), channel_id=1, source_target_pairs={{0,8},{8,16},{16,24},{24,0},{1,9},{9,17},{17,25},{25,1},{2,10},{10... | collective-permute-start | bytes 294920 | tf_op jit(solution)/shard_map/ppermute | solution.py:49
  81.3 5.7 %collective-permute-start.1 = (bf16[48,1024]{1,0:T(8,128)(2,1)S(1)}, bf16[48,1024]{1,0:T(8,128)(2,1)S(1)}, u32[]{:S(2)}, u32[]{:S(2)}) collective-permute-start(bf16[48,1024]{1,0:T(8,128)(2,1)S(1)} %collective-permute-done), channel_id=1, source_target_pairs={{0,8},{8,16},{16,24},{24,0},{1,9},{9,17},{17,25},{25,1},{2,10},{10... | collective-permute-start | bytes 294920 | tf_op jit(solution)/shard_map/ppermute | solution.py:49
  87.0 5.5 %collective-permute-start.2 = (bf16[48,1024]{1,0:T(8,128)(2,1)S(1)}, bf16[48,1024]{1,0:T(8,128)(2,1)S(1)}, u32[]{:S(2)}, u32[]{:S(2)}) collective-permute-start(bf16[48,1024]{1,0:T(8,128)(2,1)S(1)} %collective-permute-done.1), channel_id=1, source_target_pairs={{0,8},{8,16},{16,24},{24,0},{1,9},{9,17},{17,25},{25,1},{2,10},{10... | collective-permute-start | bytes 294920 | tf_op jit(solution)/shard_map/ppermute | solution.py:49
  94.3 71.6 %all-to-all-start.1 = ((bf16[48,8,1,1024]{3,0,2,1:T(8,128)(2,1)}), bf16[48,8,1,1024]{3,0,2,1:T(8,128)(2,1)S(1)}, u32[]{:S(2)}, u32[]{:S(2)}) async-start(bf16[48,8,1,1024]{3,0,2,1:T(8,128)(2,1)} %bitcast.6), calls=%async_computation.3 | async-start | bytes 1572864 | tf_op jit(solution)/shard_map/all_to_all | solution.py:59
  97.9 49.6 %reduce-scatter.5.cloned.1.call-start = ((), (), s32[]{:S(2)}) async-start(), calls=%async_computation.8 | async-start | bytes 491520 | tf_op jit(solution)/shard_map/reduce_scatter | solution.py:27
  165.9 33.8 %all-to-all-start = ((bf16[48,4,2,1,1024]{4,2,0,3,1:T(2,128)(2,1)}), bf16[48,4,2,1,1024]{4,2,0,3,1:T(2,128)(2,1)S(1)}, u32[]{:S(2)}, u32[]{:S(2)}) async-start(bf16[48,4,2,1,1024]{4,2,0,3,1:T(2,128)(2,1)} %copy.15), calls=%async_computation.1 | async-start | bytes 1572864 | tf_op jit(solution)/shard_map/all_to_all | solution.py:36
  169.4 66.1 %reduce-scatter.9.cloned.1.call-start = ((), (), s32[]{:S(2)}) async-start(), calls=%async_computation.10 | async-start | bytes 1769472 | tf_op jit(solution)/shard_map/reduce_scatter | solution.py:44
  169.8 29.9 %copy-start.2 = (bf16[48,4096]{1,0:T(8,128)(2,1)}, bf16[48,4096]{1,0:T(8,128)(2,1)S(1)}, u32[]{:S(2)}) copy-start(bf16[48,4096]{1,0:T(8,128)(2,1)S(1)} %fusion.2) | copy-start | bytes 1179652
  169.9 158.1 %copy-start.4 = (f32[48]{0:T(128)S(1)}, f32[48]{0:T(128)}, u32[]{:S(2)}) copy-start(f32[48]{0:T(128)} %param.13) | copy-start | bytes 580
  199.5 61.9 %reduce-scatter.11.cloned.1.call-start = ((), (), s32[]{:S(2)}) async-start(), calls=%async_computation.11 | async-start | bytes 491520 | tf_op jit(solution)/shard_map/reduce_scatter | solution.py:27
  225.8 36.5 %copy-start.3 = (f32[48,4096]{1,0:T(8,128)}, f32[48,4096]{1,0:T(8,128)S(1)}, u32[]{:S(2)}) copy-start(f32[48,4096]{1,0:T(8,128)S(1)} %fusion.33) | copy-start | bytes 2359300
  236.4 25.9 %collective-permute-start.3 = (bf16[48,1024]{1,0:T(8,128)(2,1)S(1)}, bf16[48,1024]{1,0:T(8,128)(2,1)S(1)}, u32[]{:S(2)}, u32[]{:S(2)}) collective-permute-start(bf16[48,1024]{1,0:T(8,128)(2,1)S(1)} %convert_element_type.71), channel_id=1, source_target_pairs={{0,8},{8,16},{16,24},{24,0},{1,9},{9,17},{17,25},{25,1},{2,10},{10... | collective-permute-start | bytes 294920 | tf_op jit(solution)/shard_map/ppermute | solution.py:49
  262.3 22.5 %collective-permute-start.4 = (bf16[48,1024]{1,0:T(8,128)(2,1)S(1)}, bf16[48,1024]{1,0:T(8,128)(2,1)}, u32[]{:S(2)}, u32[]{:S(2)}) collective-permute-start(bf16[48,1024]{1,0:T(8,128)(2,1)S(1)} %collective-permute-done.3), channel_id=1, source_target_pairs={{0,8},{8,16},{16,24},{24,0},{1,9},{9,17},{17,25},{25,1},{2,10},{10... | collective-permute-start | bytes 294920 | tf_op jit(solution)/shard_map/ppermute | solution.py:49
  281.3 19.7 %all-to-all-start.3 = ((bf16[48,4,2,1,1024]{4,2,0,3,1:T(2,128)(2,1)}), bf16[48,4,2,1,1024]{4,2,0,3,1:T(2,128)(2,1)S(1)}, u32[]{:S(2)}, u32[]{:S(2)}) async-start(bf16[48,4,2,1,1024]{4,2,0,3,1:T(2,128)(2,1)} %copy.21), calls=%async_computation.7 | async-start | bytes 1572864 | tf_op jit(solution)/shard_map/all_to_all | solution.py:36
  284.8 14.6 %collective-permute-start.5 = (bf16[48,1024]{1,0:T(8,128)(2,1)}, bf16[48,1024]{1,0:T(8,128)(2,1)S(1)}, u32[]{:S(2)}, u32[]{:S(2)}) collective-permute-start(bf16[48,1024]{1,0:T(8,128)(2,1)} %collective-permute-done.4), channel_id=1, source_target_pairs={{0,8},{8,16},{16,24},{24,0},{1,9},{9,17},{17,25},{25,1},{2,10},{10... | collective-permute-start | bytes 294920 | tf_op jit(solution)/shard_map/ppermute | solution.py:49
  302.0 25.9 %all-to-all-start.2 = ((bf16[48,8,1,1024]{3,0,2,1:T(8,128)(2,1)}), bf16[48,8,1,1024]{3,0,2,1:T(8,128)(2,1)S(1)}, u32[]{:S(2)}, u32[]{:S(2)}) async-start(bf16[48,8,1,1024]{3,0,2,1:T(8,128)(2,1)} %bitcast.53), calls=%async_computation.5 | async-start | bytes 1572864 | tf_op jit(solution)/shard_map/all_to_all | solution.py:59
Sparse Core Ops, SparseCore 0:
  36.9 36.8 reduce-scatter.6
  199.6 35.8 reduce-scatter.8
  238.3 23.0 reduce-scatter.10
Sparse Core Ops, SparseCore 1:
  122.2 25.2 reduce-scatter.4
